TPU v7x, 128 devices: a whole 4x4x4 slice. The times are simulated.
128 devices in a mesh: ctx: 16 (over z_hi, x, core), head: 8 (over z_lo, y).
Axes of the slice: x: 4, y: 4, z: 4 (z_hi: 2, z_lo: 2; z = z_hi * 2 + z_lo), core: 2. Of those that a mesh axis runs over, the one named last changes fastest.
Arguments:
- tokens: bfloat16 [16384, 4096], P('ctx', 'head'), may hold values from -23 to 23
- proj_weight: bfloat16 [4096, 32, 384], P(None, 'head'), may hold values from -1 to 1
- partner_shard: int32 [32, 256, 3], P('head'), may hold values from 0 to 15, all different within a row; in each aligned block of 16 rows (0 to 15, 16 to 31, ..., all dimensions but the last counted through in order) at most 6 rows name the same one
- partner_block: int32 [32, 256, 3], P('head'), may hold values from 0 to 15
Outputs:
- attended: bfloat16 [16384, 32, 128], P('ctx', 'head')
Inputs may be any that keep to these rules, and one draw needn't show every extreme that they name: `partner_shard`: the 3 entries of one row differ. For each head, within each aligned run of 16 block rows, no value is named more than 6 times, and some runs name one value exactly 6 times.
All inputs are finite; a program needn't handle non-finite values.
Results may differ from a plain program's by a relative error of at most 0.008.
Values may be sent and summed in bfloat16 or wider, within the bound.
A program may use at most 192 MiB of HBM per device.

v0:
```python
import jax
import jax.numpy as jnp
from jax import lax
from jax.sharding import PartitionSpec as P

HEAD_DIMENSION = 128
BLK = 64
GLOB = 2
RAND = 3


def padded_2(cells, sides, width):
    for axis, dim in sides:
        count = lax.axis_size(axis)
        head = lax.slice_in_dim(cells, 0, width, axis=dim)
        tail = lax.slice_in_dim(cells, cells.shape[dim] - width, cells.shape[dim], axis=dim)
        cells = jnp.concatenate(
            [
                lax.ppermute(tail, axis, [(i, (i + 1) % count) for i in range(count)]),
                cells,
                lax.ppermute(head, axis, [((i + 1) % count, i) for i in range(count)]),
            ],
            axis=dim,
        )
    return cells


def from_root(block, axis, holder):
    block = jnp.where(lax.axis_index(axis) == holder, block, jnp.zeros_like(block))
    return lax.psum(block, axis)


def combined_all(part, axis, combine):
    gathered = jax.tree.map(lambda a: lax.all_gather(a, axis), part)

    def take(source):
        return jax.tree.map(lambda a: lax.dynamic_index_in_dim(a, source, 0, False), gathered)

    return lax.fori_loop(
        1, lax.axis_size(axis), lambda source, state: combine(state, take(source)), take(0)
    )


def per_device(tokens, proj_weight, partner_shard, partner_block):
    row_count = tokens.shape[0]
    head_count = proj_weight.shape[1]
    blocks = row_count // BLK
    shard_index = lax.axis_index("ctx")
    inverse_root_scale = HEAD_DIMENSION ** (-0.5)
    packed = jnp.einsum(
        "td,dhe->the",
        lax.all_gather(tokens, "head", axis=1, tiled=True),
        proj_weight,
        preferred_element_type=jnp.float32,
    ).astype(jnp.bfloat16)
    queries = packed[..., :HEAD_DIMENSION]
    keyval = packed[..., HEAD_DIMENSION:]
    padded = padded_2(keyval, (("ctx", 0),), BLK)
    window = jnp.concatenate(
        [
            padded[0:row_count].reshape(blocks, BLK, head_count, 2 * HEAD_DIMENSION),
            padded[BLK : row_count + BLK].reshape(blocks, BLK, head_count, 2 * HEAD_DIMENSION),
            padded[2 * BLK : row_count + 2 * BLK].reshape(
                blocks, BLK, head_count, 2 * HEAD_DIMENSION
            ),
        ],
        axis=1,
    )
    global_pack = from_root(packed[: GLOB * BLK], "ctx", 0)
    global_query = global_pack[..., :HEAD_DIMENSION]
    global_keyval = global_pack[..., HEAD_DIMENSION:]
    row_total = blocks * RAND
    owners = lax.dynamic_slice_in_dim(partner_shard, shard_index * blocks, blocks, 1).reshape(
        head_count, row_total
    )
    offsets = lax.dynamic_slice_in_dim(partner_block, shard_index * blocks, blocks, 1).reshape(
        head_count, row_total
    )
    partner_index = owners * blocks + offsets
    block_rows = lax.all_gather(keyval, "ctx", axis=0, tiled=True)
    piece_blocks = block_rows.shape[0] // BLK
    piece_hot = (partner_index[..., None] == jnp.arange(piece_blocks)).astype(jnp.bfloat16)
    blocked = block_rows.reshape(piece_blocks, BLK, head_count, 2 * HEAD_DIMENSION)
    fetched = jnp.einsum(
        "hrb,bthe->hrte", piece_hot, blocked, preferred_element_type=jnp.float32
    ).astype(jnp.bfloat16)
    remote = fetched
    remote = remote.reshape(head_count, blocks, RAND * BLK, 2 * HEAD_DIMENSION)
    blocked_query_rows = queries.reshape(blocks, BLK, head_count, HEAD_DIMENSION)
    window_scores = jnp.einsum(
        "bqhd,bkhd->bhqk",
        blocked_query_rows,
        window[..., :HEAD_DIMENSION],
        preferred_element_type=jnp.float32,
    )
    global_scores = jnp.einsum(
        "bqhd,khd->bhqk",
        blocked_query_rows,
        global_keyval[..., :HEAD_DIMENSION],
        preferred_element_type=jnp.float32,
    )
    remote_scores = jnp.einsum(
        "bqhd,hbkd->bhqk",
        blocked_query_rows,
        remote[..., :HEAD_DIMENSION],
        preferred_element_type=jnp.float32,
    )
    logit_scores = (
        jnp.concatenate([window_scores, global_scores, remote_scores], axis=-1) * inverse_root_scale
    )
    softmax_weight_matrix = jax.nn.softmax(logit_scores, axis=-1).astype(jnp.bfloat16)
    width_window = 3 * BLK
    width_global = GLOB * BLK
    context = jnp.einsum(
        "bhqk,bkhd->bqhd",
        softmax_weight_matrix[..., :width_window],
        window[..., HEAD_DIMENSION:],
        preferred_element_type=jnp.float32,
    )
    context = context + jnp.einsum(
        "bhqk,khd->bqhd",
        softmax_weight_matrix[..., width_window : width_window + width_global],
        global_keyval[..., HEAD_DIMENSION:],
        preferred_element_type=jnp.float32,
    )
    context = context + jnp.einsum(
        "bhqk,hbkd->bqhd",
        softmax_weight_matrix[..., width_window + width_global :],
        remote[..., HEAD_DIMENSION:],
        preferred_element_type=jnp.float32,
    )
    sparse_attention_output = context.astype(jnp.bfloat16).reshape(
        row_count, head_count, HEAD_DIMENSION
    )
    lead_scores = (
        jnp.einsum(
            "qhd,khd->hqk",
            global_query,
            keyval[..., :HEAD_DIMENSION],
            preferred_element_type=jnp.float32,
        )
        * inverse_root_scale
    )
    maxima = jnp.max(lead_scores, axis=-1)
    exp_terms = jnp.exp(lead_scores - maxima[..., None])
    totals = jnp.sum(exp_terms, axis=-1)
    summed = jnp.einsum(
        "hqk,khd->hqd",
        exp_terms,
        keyval[..., HEAD_DIMENSION:].astype(jnp.float32),
        precision=lax.Precision.HIGHEST,
    )

    def combine(first, second):
        max_first, total_first, sum_first = first
        max_second, total_second, sum_second = second
        larger = jnp.maximum(max_first, max_second)
        factor_first = jnp.exp(max_first - larger)
        factor_second = jnp.exp(max_second - larger)
        return (
            larger,
            total_first * factor_first + total_second * factor_second,
            sum_first * factor_first[..., None] + sum_second * factor_second[..., None],
        )

    maxima, totals, summed = combined_all((maxima, totals, summed), "ctx", combine)
    global_out = jnp.transpose((summed / totals[..., None]).astype(jnp.bfloat16), (1, 0, 2))
    head_rows = jnp.where(shard_index == 0, global_out, sparse_attention_output[: GLOB * BLK])
    return jnp.concatenate([head_rows, sparse_attention_output[GLOB * BLK :]], axis=0)


def solution(mesh):
    in_specs = (
        P("ctx", "head"),
        P(None, "head", None),
        P("head", None, None),
        P("head", None, None),
    )
    out_specs = P("ctx", "head", None)
    return jax.shard_map(
        per_device, mesh=mesh, in_specs=in_specs, out_specs=out_specs, check_vma=False
    )
```

profile of v0, /device:TPU:1, one launch (start us, length us, event | category | flops | bytes accessed | tf_op | source)
XLA Modules:
  0.0 600.8 jit_solution(12266525961735290425)
XLA Ops:
  6.5 0.7 all-gather.9.cloned.1.call-update
  7.3 96.7 %all-gather.9.cloned.1.call-done = bf16[1024,4096]{1,0:T(8,128)(2,1)} async-done(((bf16[1024,512]{1,0:T(8,128)(2,1)}), bf16[1024,4096]{1,0:T(8,128)(2,1)}) %all-gather.9.cloned.1.call-update) | async-done | bytes 8388624 | tf_op jit(solution)/shard_map/all_gather | solution.py:52
  104.0 18.3 %fusion.22 = bf16[1024,4,384]{2,0,1:T(8,128)(2,1)S(1)} fusion(bf16[4096,4,384]{2,1,0:T(4,128)(2,1)} %param.7, bf16[1024,4096]{1,0:T(8,128)(2,1)} %all-gather.9.cloned.1.call-done), kind=kOutput, calls=%fused_computation.29 | convolution fusion | flops 12886474752 | bytes 24117248 | tf_op jit(solution)/shard_map/td,dhe->the/dot_general | solution.py:50
  122.3 0.8 slice_select_fusion
  123.2 138.2 %all-reduce.2.cloned.1.call-done = bf16[128,4,384]{2,0,1:T(8,128)(2,1)} async-done(((bf16[128,4,384]{2,0,1:T(8,128)(2,1)}), bf16[128,4,384]{2,0,1:T(8,128)(2,1)}) %all-reduce.2.cloned.1.call-update) | async-done | bytes 393232 | tf_op jit(solution)/shard_map/psum | solution.py:30
  261.4 1.4 multiply_reduce_fusion
  262.8 1.3 copy-done.1
  264.1 2.2 fusion.30
  266.4 1.5 slice.118
  267.9 1.8 fusion.56
  269.7 0.7 collective-permute-start.1
  270.4 0.8 dynamic-slice_add_fusion
  271.3 1.3 slice.116
  272.6 1.4 collective-permute-done.1
  274.4 5.0 pad_maximum_fusion
  279.4 3.4 fusion.54
  282.8 4.1 fusion.20
  286.9 25.5 %all-gather.3 = f32[16,4,128]{2,1,0:T(4,128)S(1)} all-gather(f32[1,4,128]{2,1,0:T(4,128)S(1)} %bitcast.75), channel_id=2, replica_groups=mesh['ctx'=16,'head'=8] {'ctx'}, dimensions={0}, use_global_device_ids=true | all-gather | bytes 34816 | tf_op jit(solution)/shard_map/all_gather | solution.py:34
  312.9 19.5 %all-gather.4 = f32[16,4,128]{2,1,0:T(4,128)S(1)} all-gather(f32[1,4,128]{2,1,0:T(4,128)S(1)} %bitcast.76), channel_id=3, replica_groups=mesh['ctx'=16,'head'=8] {'ctx'}, dimensions={0}, use_global_device_ids=true | all-gather | bytes 34816 | tf_op jit(solution)/shard_map/all_gather | solution.py:34
  332.4 1.3 convolution_bitcast_fusion
  333.8 1.0 slice.115
  334.8 19.0 %while.19 = (s32[]{:T(128)}, f32[4,128]{1,0:T(4,128)S(1)}, f32[4,128]{1,0:T(4,128)S(1)}, f32[4,128,128]{2,1,0:T(8,128)S(1)}, f32[16,4,128]{2,1,0:T(4,128)S(1)}, ...) while((s32[]{:T(128)}, f32[4,128]{1,0:T(4,128)S(1)}, ...), condition=%wide.region_4.5_spmd, body=%wide.region_3.4_spmd.sunk | while | flops 199685 | bytes 807063 | solution.py:39
  334.8 1.3 fusion.61
  336.1 1.2 fusion.61
  337.4 1.2 fusion.61
  338.7 1.3 fusion.61
  340.0 1.2 fusion.61
  341.2 1.2 fusion.61
  342.5 1.2 fusion.61
  343.8 1.2 fusion.61
  345.0 1.2 fusion.61
  346.3 1.2 fusion.61
  347.5 1.2 fusion.61
  348.8 1.2 fusion.61
  350.1 1.2 fusion.61
  351.3 1.2 fusion.61
  352.6 1.2 fusion.61
  353.8 158.4 %all-gather.11.cloned.1.call-done = bf16[16384,4,256]{2,0,1:T(8,128)(2,1)} async-done(((bf16[1024,4,256]{2,0,1:T(8,128)(2,1)}), bf16[16384,4,256]{2,0,1:T(8,128)(2,1)}) %all-gather.11.cloned.1.call-update) | async-done | bytes 33554448 | tf_op jit(solution)/shard_map/all_gather | solution.py:80
  512.2 34.4 %fusion.11 = bf16[4,48,64,256]{3,1,2,0:T(8,128)(2,1)S(1)} fusion(bf16[256,64,4,256]{3,1,0,2:T(8,128)(2,1)} %bitcast.65, s32[4,48]{1,0:T(4,128)S(1)} %add.84), kind=kOutput, calls=%fused_computation.20 | convolution fusion | flops 1613807616 | bytes 39846656 | tf_op jit(solution)/shard_map/hrb,bthe->hrte/dot_general | solution.py:84
  546.6 2.5 copy.42
  549.1 1.8 fusion.55
  550.9 4.1 fusion.18
  555.0 28.1 %fusion.57 = (f32[16,4,64]{2,1,0:T(4,128)S(1)}, f32[16,4,64,512]{3,2,1,0:T(8,128)}) fusion(f32[16,4,64,192]{3,2,1,0:T(8,128)} %fusion.18, f32[16,4,64,128]{3,2,1,0:T(8,128)S(1)} %convolution_bitcast_fusion, f32[16,4,64,192]{3,2,1,0:T(8,128)S(1)} %copy-done.5), kind=kOutput, calls=%fused_computation.71 | output fusion | flops 10486271 | bytes 16793600 | tf_op jit(solution)/shard_map/sub | solution.py:111
  583.1 4.1 divide_convert_fusion
  587.1 1.3 fusion.14
  588.4 1.6 fusion.36
  590.4 1.4 fusion.29
  592.2 1.8 copy.48
  (48 shorter events, 2.3 us)
Async XLA Ops:
  6.5 97.4 %all-gather.9.cloned.1.call-start = ((), (), s32[]{:S(2)}) async-start(), calls=%async_computation | async-start | bytes 9437184 | tf_op jit(solution)/shard_map/all_gather | solution.py:52
  7.3 254.2 %all-reduce.2.cloned.1.call-start = ((), (), s32[]{:S(2)}) async-start(), calls=%async_computation.1 | async-start | bytes 786432 | tf_op jit(solution)/shard_map/psum | solution.py:30
  122.3 144.1 %copy-start.4 = (bf16[1024,4,384]{2,0,1:T(8,128)(2,1)}, bf16[1024,4,384]{2,0,1:T(8,128)(2,1)S(1)}, u32[]{:S(2)}) copy-start(bf16[1024,4,384]{2,0,1:T(8,128)(2,1)S(1)} %fusion.22) | copy-start | bytes 9437188
  123.2 210.6 %all-gather.13.cloned.1.call-start = ((), (), s32[]{:S(2)}) async-start(), calls=%async_computation.3 | async-start | bytes 4456448 | tf_op jit(solution)/shard_map/all_gather | solution.py:34
  262.8 1.3 copy-start.1
  266.3 245.9 %all-gather.11.cloned.1.call-start = ((), (), s32[]{:S(2)}) async-start(), calls=%async_computation.2 | async-start | bytes 35651584 | tf_op jit(solution)/shard_map/all_gather | solution.py:80
  267.9 6.2 %copy-start = (bf16[1024,4,256]{2,0,1:T(8,128)(2,1)S(1)}, bf16[1024,4,256]{2,0,1:T(8,128)(2,1)}, u32[]{:S(2)}) copy-start(bf16[1024,4,256]{2,0,1:T(8,128)(2,1)} %slice.118) | copy-start | bytes 6291460
  269.7 2.9 collective-permute-start
  269.7 4.4 collective-permute-start.1
  282.8 29.6 %copy-start.2 = (f32[4,128,1024]{2,1,0:T(8,128)S(1)}, f32[4,128,1024]{2,1,0:T(8,128)}, u32[]{:S(2)}) copy-start(f32[4,128,1024]{2,1,0:T(8,128)} %copy-done.1) | copy-start | bytes 6291460
  550.9 4.1 copy-start.5
  588.4 2.0 copy-start.3
Sparse Core Ops, SparseCore 0:
  9.0 94.9 all-gather.8
  123.3 138.0 all-reduce.1
  266.4 57.4 all-gather.12
  326.3 185.8 all-gather.10
where the time goes:
time: 610 us; the launch traced here: 601 us
  waiting for transfers between devices  396 us (65%)
  matrix products  70 us (11%)
  other arithmetic  58.3 us (10%)
  blocking collectives  45 us (7%)
  local copies, waits for them, and re-layouts  17.1 us (3%)
  between operations  13.6 us (2%)
    all_gather x1, waiting for transfers between devices, per_device(): block_rows = lax.all_gather(keyval, 'ctx', axis=0, tiled=True)  158 us
    psum x1, waiting for transfers between devices, from_root(): return lax.psum(block, axis)  138 us
    all_gather x1, waiting for transfers between devices, per_device(): lax.all_gather(tokens, 'head', axis=1, tiled=True)  96.7 us
    all_gather x2, blocking collectives, combined_all(): gathered = jax.tree.map(lambda a: lax.all_gather(a, axis), part)  45 us
    dot_general x1, matrix products, per_device(): jnp.einsum('hrb,bthe->hrte', piece_hot, blocked, preferred_element_type=j...  34.4 us
    sub x1, other arithmetic, per_device(): jax.nn.softmax(logit_scores, axis=-1).astype(jnp.bfloat16)  28.1 us
    dot_general x1, matrix products, per_device(): jnp.einsum('td,dhe->the', lax.all_gather(tokens, 'head', axis=1, tiled=Tr...  18.3 us
    add x15, other arithmetic, combine(): sum_first * factor_first[..., None] + sum_second * factor_second[..., None]  18.2 us
  transfers between devices with their start and end apart: 6, of which 4 were waited for; matrix products, arithmetic and copies ran while one was open for 7% of the time, Pallas kernels for 0%

commit v1 on v0

--- a/solution.py
+++ b/solution.py
@@ -27,7 +27,7 @@
 
 def from_root(block, axis, holder):
     block = jnp.where(lax.axis_index(axis) == holder, block, jnp.zeros_like(block))
-    return lax.psum(block, axis)
+    return jnp.sum(jax.lax.all_gather(block, axis_name=axis), axis=0)
 
 
 def combined_all(part, axis, combine):

time: 610 us -> 534 us (0.88)
  waiting for transfers between devices: 396 us -> 319 us
    psum x1 -> x0, waiting for transfers between devices: 138 us -> none  [from_root(): return lax.psum(block, axis)]
    all_gather x0 -> x1, waiting for transfers between devices: none -> 63.2 us  [from_root(): return jnp.sum(jax.lax.all_gather(block, axis_name=axis), axis=0)]
  transfers between devices with their start and end apart: 6 -> 6, of which waited for: 4 -> 4; matrix products, arithmetic and copies ran while one was open for 7% -> 8% of each run, Pallas kernels for 0% -> 0%
where the time goes in v1:
time: 534 us; the launch traced here: 527 us
  waiting for transfers between devices  319 us (60%)
  matrix products  69 us (13%)
  other arithmetic  62.2 us (12%)
  blocking collectives  44.1 us (8%)
  local copies, waits for them, and re-layouts  17.4 us (3%)
  between operations  13.6 us (3%)
    all_gather x1, waiting for transfers between devices, per_device(): block_rows = lax.all_gather(keyval, 'ctx', axis=0, tiled=True)  156 us
    all_gather x1, waiting for transfers between devices, per_device(): lax.all_gather(tokens, 'head', axis=1, tiled=True)  96.7 us
    all_gather x1, waiting for transfers between devices, from_root(): return jnp.sum(jax.lax.all_gather(block, axis_name=axis), axis=0)  63.2 us
    all_gather x2, blocking collectives, combined_all(): gathered = jax.tree.map(lambda a: lax.all_gather(a, axis), part)  44.1 us
    dot_general x1, matrix products, per_device(): jnp.einsum('hrb,bthe->hrte', piece_hot, blocked, preferred_element_type=j...  34.4 us
    sub x1, other arithmetic, per_device(): jax.nn.softmax(logit_scores, axis=-1).astype(jnp.bfloat16)  28.1 us
    dot_general x1, matrix products, per_device(): jnp.einsum('td,dhe->the', lax.all_gather(tokens, 'head', axis=1, tiled=Tr...  18.3 us
    add x15, other arithmetic, combine(): sum_first * factor_first[..., None] + sum_second * factor_second[..., None]  18.2 us
  transfers between devices with their start and end apart: 6, of which 4 were waited for; matrix products, arithmetic and copies ran while one was open for 8% of the time, Pallas kernels for 0%

profile of v1, /device:TPU:1, one launch (start us, length us, event | category | flops | bytes accessed | tf_op | source)
XLA Modules:
  0.0 527.0 jit_solution(959025131136193785)
XLA Ops:
  6.5 0.7 all-gather.11.cloned.1.call-update
  7.3 96.7 %all-gather.11.cloned.1.call-done = bf16[1024,4096]{1,0:T(8,128)(2,1)} async-done(((bf16[1024,512]{1,0:T(8,128)(2,1)}), bf16[1024,4096]{1,0:T(8,128)(2,1)}) %all-gather.11.cloned.1.call-update) | async-done | bytes 8388624 | tf_op jit(solution)/shard_map/all_gather | solution.py:52
  104.0 18.3 %fusion.22 = bf16[1024,4,384]{2,0,1:T(8,128)(2,1)S(1)} fusion(bf16[4096,4,384]{2,1,0:T(4,128)(2,1)} %param.7, bf16[1024,4096]{1,0:T(8,128)(2,1)} %all-gather.11.cloned.1.call-done), kind=kOutput, calls=%fused_computation.29 | convolution fusion | flops 12886474752 | bytes 24117248 | tf_op jit(solution)/shard_map/td,dhe->the/dot_general | solution.py:50
  122.3 0.9 slice_select_fusion
  123.2 63.2 %all-gather.15.cloned.1.call-done = bf16[2048,4,384]{2,0,1:T(8,128)(2,1)} async-done(((bf16[128,4,384]{2,0,1:T(8,128)(2,1)}), bf16[2048,4,384]{2,0,1:T(8,128)(2,1)}) %all-gather.15.cloned.1.call-update) | async-done | bytes 6291472 | tf_op jit(solution)/shard_map/all_gather | solution.py:30
  186.4 3.9 reduce_sum.30
  190.9 1.3 copy-done.1
  192.2 2.2 fusion.30
  194.4 1.5 slice.118
  196.0 1.8 fusion.56
  197.8 0.9 collective-permute-start
  199.0 0.8 dynamic-slice_add_fusion
  200.0 1.3 slice.116
  201.3 2.1 collective-permute-done.1
  203.7 5.0 pad_maximum_fusion
  208.7 3.4 fusion.54
  212.1 4.1 fusion.20
  216.2 24.3 %all-gather.4 = f32[16,4,128]{2,1,0:T(4,128)S(1)} all-gather(f32[1,4,128]{2,1,0:T(4,128)S(1)} %bitcast.77), channel_id=3, replica_groups=mesh['ctx'=16,'head'=8] {'ctx'}, dimensions={0}, use_global_device_ids=true | all-gather | bytes 34816 | tf_op jit(solution)/shard_map/all_gather | solution.py:34
  240.9 19.9 %all-gather.5 = f32[16,4,128]{2,1,0:T(4,128)S(1)} all-gather(f32[1,4,128]{2,1,0:T(4,128)S(1)} %bitcast.78), channel_id=4, replica_groups=mesh['ctx'=16,'head'=8] {'ctx'}, dimensions={0}, use_global_device_ids=true | all-gather | bytes 34816 | tf_op jit(solution)/shard_map/all_gather | solution.py:34
  260.8 1.4 convolution_bitcast_fusion
  262.2 1.0 slice.115
  263.2 18.9 %while.19 = (s32[]{:T(128)}, f32[4,128]{1,0:T(4,128)S(1)}, f32[4,128]{1,0:T(4,128)S(1)}, f32[4,128,128]{2,1,0:T(8,128)S(1)}, f32[16,4,128]{2,1,0:T(4,128)S(1)}, ...) while((s32[]{:T(128)}, f32[4,128]{1,0:T(4,128)S(1)}, ...), condition=%wide.region_4.5_spmd, body=%wide.region_3.4_spmd.sunk | while | flops 199685 | bytes 807063 | solution.py:39
  263.3 1.2 fusion.61
  264.6 1.3 fusion.61
  265.9 1.2 fusion.61
  267.1 1.2 fusion.61
  268.4 1.2 fusion.61
  269.6 1.2 fusion.61
  270.9 1.2 fusion.61
  272.2 1.2 fusion.61
  273.4 1.2 fusion.61
  274.7 1.2 fusion.61
  275.9 1.2 fusion.61
  277.2 1.2 fusion.61
  278.4 1.2 fusion.61
  279.7 1.2 fusion.61
  281.0 1.2 fusion.61
  282.2 156.3 %all-gather.13.cloned.1.call-done = bf16[16384,4,256]{2,0,1:T(8,128)(2,1)} async-done(((bf16[1024,4,256]{2,0,1:T(8,128)(2,1)}), bf16[16384,4,256]{2,0,1:T(8,128)(2,1)}) %all-gather.13.cloned.1.call-update) | async-done | bytes 33554448 | tf_op jit(solution)/shard_map/all_gather | solution.py:80
  438.4 34.4 %fusion.11 = bf16[4,48,64,256]{3,1,2,0:T(8,128)(2,1)S(1)} fusion(bf16[256,64,4,256]{3,1,0,2:T(8,128)(2,1)} %bitcast.66, s32[4,48]{1,0:T(4,128)S(1)} %add.82), kind=kOutput, calls=%fused_computation.20 | convolution fusion | flops 1613807616 | bytes 39846656 | tf_op jit(solution)/shard_map/hrb,bthe->hrte/dot_general | solution.py:84
  472.8 2.5 copy.42
  475.3 1.8 fusion.55
  477.1 4.1 fusion.18
  481.2 28.1 %fusion.57 = (f32[16,4,64]{2,1,0:T(4,128)S(1)}, f32[16,4,64,512]{3,2,1,0:T(8,128)}) fusion(f32[16,4,64,192]{3,2,1,0:T(8,128)} %fusion.18, f32[16,4,64,128]{3,2,1,0:T(8,128)S(1)} %convolution_bitcast_fusion, f32[16,4,64,192]{3,2,1,0:T(8,128)S(1)} %copy-done.5), kind=kOutput, calls=%fused_computation.71 | output fusion | flops 10486271 | bytes 16793600 | tf_op jit(solution)/shard_map/sub | solution.py:111
  509.3 4.1 divide_convert_fusion
  513.3 1.4 fusion.36
  514.8 1.3 fusion.14
  516.6 1.4 fusion.29
  518.5 1.8 copy.48
  (51 shorter events, 3.4 us)
Async XLA Ops:
  6.5 97.4 %all-gather.11.cloned.1.call-start = ((), (), s32[]{:S(2)}) async-start(), calls=%async_computation | async-start | bytes 9437184 | tf_op jit(solution)/shard_map/all_gather | solution.py:52
  7.3 179.2 %all-gather.15.cloned.1.call-start = ((), (), s32[]{:S(2)}) async-start(), calls=%async_computation.2 | async-start | bytes 6684672 | tf_op jit(solution)/shard_map/all_gather | solution.py:30
  122.3 72.1 %copy-start.4 = (bf16[1024,4,384]{2,0,1:T(8,128)(2,1)}, bf16[1024,4,384]{2,0,1:T(8,128)(2,1)S(1)}, u32[]{:S(2)}) copy-start(bf16[1024,4,384]{2,0,1:T(8,128)(2,1)S(1)} %fusion.22) | copy-start | bytes 9437188
  123.2 139.0 %all-gather.17.cloned.1.call-start = ((), (), s32[]{:S(2)}) async-start(), calls=%async_computation.3 | async-start | bytes 4456448 | tf_op jit(solution)/shard_map/all_gather | solution.py:34
  190.4 4.0 copy-start.6
  190.9 1.3 copy-start.1
  194.4 244.1 %all-gather.13.cloned.1.call-start = ((), (), s32[]{:S(2)}) async-start(), calls=%async_computation.1 | async-start | bytes 35651584 | tf_op jit(solution)/shard_map/all_gather | solution.py:80
  195.9 7.4 %copy-start = (bf16[1024,4,256]{2,0,1:T(8,128)(2,1)S(1)}, bf16[1024,4,256]{2,0,1:T(8,128)(2,1)}, u32[]{:S(2)}) copy-start(bf16[1024,4,256]{2,0,1:T(8,128)(2,1)} %slice.118) | copy-start | bytes 6291460
  197.8 3.5 collective-permute-start
  198.7 4.7 collective-permute-start.1
  212.1 28.3 %copy-start.2 = (f32[4,128,1024]{2,1,0:T(8,128)S(1)}, f32[4,128,1024]{2,1,0:T(8,128)}, u32[]{:S(2)}) copy-start(f32[4,128,1024]{2,1,0:T(8,128)} %copy-done.1) | copy-start | bytes 6291460
  477.1 4.1 copy-start.5
  514.8 1.9 copy-start.3
Sparse Core Ops, SparseCore 0:
  9.0 94.9 all-gather.10
  123.3 63.0 all-gather.14
  194.5 55.6 all-gather.16
  252.5 185.8 all-gather.12
